TPU v7x, 32 devices: a whole 2x2x4 slice. The times are simulated.
32 devices in a mesh: group: 2 (over y), tm: 4 (over z), tensor: 2 (over x), dp: 2 (over core).
Axes of the slice: x: 2, y: 2, z: 4, core: 2. Of those that a mesh axis runs over, the one named last changes fastest.
Arguments:
- frames_in: bfloat16 [4, 3072, 1024], P(('group', 'dp'), 'tm', 'tensor'), parts along dimension 0, may hold values from -6 to 6
- in_proj: bfloat16 [2, 1024, 1024], P(None, None, 'tensor'), may hold values from -0.1875 to 0.1875
- log_rates: float32 [8, 8], P(None, 'tensor'), as said below
- angles: float32 [8, 8], P(None, 'tensor'), may hold values from -3.140625 to 3.140625
- residues: float32 [2, 8, 1024], P(None, None, 'tensor'), may hold values from -3 to 3
- skip_gain: float32 [1024], P('tensor'), may hold values from -3 to 3
- lengths: int32 [4, 4], P(('group', 'dp')), parts along dimension 0, may hold values from 1 to 1536, 3072 in all within a row
- grad_out: bfloat16 [4, 3072, 1024], P(('group', 'dp'), 'tm', 'tensor'), parts along dimension 0, may hold values from -6 to 6
Outputs:
- mixed: bfloat16 [4, 3072, 1024], P(('group', 'dp'), 'tm', 'tensor'), parts along dimension 0
- input_grad: bfloat16 [4, 3072, 1024], P(('group', 'dp'), 'tm', 'tensor'), parts along dimension 0
- proj_grad: float32 [4, 1024, 1024], P('group', None, 'tensor'), parts along dimension 0
- residue_grad: float32 [4, 8, 1024], P('group', None, 'tensor'), parts along dimension 0
- skip_grad: float32 [2048], P(('group', 'tensor')), parts along dimension 0
There are 2 independent parts, one for each index of `group`. A program takes and returns all parts, laid end to end along the dimension named above; an argument that names none is the same for every part. Nothing has to cross between parts.
Inputs may be any that keep to these rules, and one draw needn't show every extreme that they name: Each clip has at least one frame; the lengths of a stream sum to 3072. `log_rates`: each entry lies between the logarithms of 0.1 / 3072 and 0.08.
All inputs are finite; a program needn't handle non-finite values.
Results may differ from a plain program's by a relative error of at most 0.0058.
Values may be sent and summed in bfloat16 or wider, within the bound.
A program may use at most 128 MiB of HBM per device.

v0:
```python
import math
import jax
import jax.numpy as jnp
from jax import lax
from jax.sharding import PartitionSpec as P

BLOCK_LEN = 128


def carried_in(value, axis, join, neutral, backward):
    count, mine = (lax.axis_size(axis), lax.axis_index(axis))
    pieces = jax.tree.map(lambda part: lax.all_gather(part, axis), value)
    if backward:
        pieces = jax.tree.map(lambda part: part[::-1], pieces)
        mine = count - 1 - mine
    total = jax.tree.map(
        lambda part, zero: jnp.full_like(part, 0) + jnp.asarray(zero, part.dtype), value, neutral
    )

    def lap(position, total):
        longer = join(total, jax.tree.map(lambda part: part[position], pieces))
        return jax.tree.map(lambda new, old: jnp.where(position < mine, new, old), longer, total)

    return lax.fori_loop(0, count - 1, lap, total)


def compose(earlier_map, later_map):
    early_re, early_im, early_sre, early_sim = earlier_map
    late_re, late_im, late_sre, late_sim = later_map
    return (
        late_re * early_re - late_im * early_im,
        late_re * early_im + late_im * early_re,
        late_re[..., None] * early_sre - late_im[..., None] * early_sim + late_sre,
        late_re[..., None] * early_sim + late_im[..., None] * early_sre + late_sim,
    )


def shards(frames_in, in_proj, log_rates, angles, residues, skip_gain, lengths, grad_out):
    rows_dev = frames_in.shape[1]
    channels = frames_in.shape[2]
    modes_dev, heads_dev = log_rates.shape
    head_width = channels // heads_dev
    block_count = rows_dev // BLOCK_LEN
    largest_value = lax.Precision.HIGHEST
    features = lax.all_gather(frames_in, "tensor", axis=2, tiled=True)[0]
    projected = jnp.einsum("ld,kdc->klc", features, in_proj, preferred_element_type=jnp.float32)
    query_rows = projected[0].astype(jnp.bfloat16)
    signal = projected[1].astype(jnp.bfloat16)
    decay_rate = jnp.exp(log_rates)
    weight = jnp.sqrt(-jnp.expm1(-2.0 * decay_rate))
    later_idx = lax.broadcasted_iota(jnp.int32, (BLOCK_LEN, BLOCK_LEN), 0)
    earlier_idx = lax.broadcasted_iota(jnp.int32, (BLOCK_LEN, BLOCK_LEN), 1)
    causal = later_idx >= earlier_idx
    lag_steps = jnp.maximum(later_idx - earlier_idx, 0).astype(jnp.float32)
    damping = jnp.where(causal, jnp.exp(-decay_rate[:, :, None, None] * lag_steps), 0.0)
    kern_re = damping * jnp.cos(angles[:, :, None, None] * lag_steps)
    kern_im = damping * jnp.sin(angles[:, :, None, None] * lag_steps)
    exponents = jnp.arange(1, rows_dev + 1, dtype=jnp.int32).astype(jnp.float32)
    exponent_real = jnp.exp(-decay_rate[:, :, None] * exponents) * jnp.cos(
        angles[:, :, None] * exponents
    )
    exponent_imaginary = jnp.exp(-decay_rate[:, :, None] * exponents) * jnp.sin(
        angles[:, :, None] * exponents
    )
    block_re = exponent_real[:, :, :BLOCK_LEN]
    block_im = exponent_imaginary[:, :, :BLOCK_LEN]
    clip_start = jnp.cumsum(lengths[0]) - lengths[0]
    first_frame = lax.axis_index("tm") * rows_dev
    frame_ids = first_frame + jnp.arange(rows_dev, dtype=jnp.int32)
    segment = jnp.sum((frame_ids[:, None] >= clip_start[None, :]).astype(jnp.int32), axis=1) - 1
    segment_before = jnp.sum((first_frame - 1 >= clip_start).astype(jnp.int32)) - 1
    seg_blocks = segment.reshape(block_count, BLOCK_LEN)
    seg_prior = jnp.concatenate([segment_before[None], seg_blocks[:-1, -1]])
    alive_dev = (segment == segment_before).astype(jnp.float32)
    carry_re = exponent_real[:, :, -1] * alive_dev[-1]
    carry_im = exponent_imaginary[:, :, -1] * alive_dev[-1]

    def split_coeffs(coeffs):
        coefficient_real = coeffs[0].reshape(modes_dev, heads_dev, head_width) * weight[:, :, None]
        coefficient_imaginary = (
            coeffs[1].reshape(modes_dev, heads_dev, head_width) * weight[:, :, None]
        )
        return (coefficient_real, coefficient_imaginary)

    def intra(signal32, coeffs, skip_vec):
        coefficient_real, coefficient_imaginary = split_coeffs(coeffs)
        skip_row = skip_vec.reshape(heads_dev, head_width)

        def block_step(carried, element):
            state_re, state_im = carried
            block_in, block_seg, prior_seg = element
            same_clip = (block_seg[:, None] == block_seg[None, :]).astype(jnp.float32)
            alive_mask = (block_seg == prior_seg).astype(jnp.float32)[None, None, :, None]
            inner_re = jnp.einsum(
                "mhts,shd->mhtd", kern_re * same_clip, block_in, precision=largest_value
            )
            inner_im = jnp.einsum(
                "mhts,shd->mhtd", kern_im * same_clip, block_in, precision=largest_value
            )
            aggregate_real = inner_re + alive_mask * (
                block_re[..., None] * state_re[:, :, None, :]
                - block_im[..., None] * state_im[:, :, None, :]
            )
            aggregate_imaginary = inner_im + alive_mask * (
                block_re[..., None] * state_im[:, :, None, :]
                + block_im[..., None] * state_re[:, :, None, :]
            )
            output = (
                skip_row * block_in
                + jnp.einsum(
                    "ywo,ywlo->lwo", coefficient_real, aggregate_real, precision=largest_value
                )
                - jnp.einsum(
                    "ywo,ywlo->lwo",
                    coefficient_imaginary,
                    aggregate_imaginary,
                    precision=largest_value,
                )
            )
            return ((aggregate_real[:, :, -1, :], aggregate_imaginary[:, :, -1, :]), output)

        initial = jnp.zeros((modes_dev, heads_dev, head_width), jnp.float32)
        blocks_in = signal32.reshape(block_count, BLOCK_LEN, heads_dev, head_width)
        final_state, outputs = lax.scan(
            jax.checkpoint(block_step), (initial, initial), (blocks_in, seg_blocks, seg_prior)
        )
        return (outputs.reshape(rows_dev, heads_dev, head_width), final_state)

    def carry_part(coeffs, enter_re, enter_im):
        coefficient_real, coefficient_imaginary = split_coeffs(coeffs)
        blended_real = coefficient_real * enter_re - coefficient_imaginary * enter_im
        blended_imaginary = coefficient_real * enter_im + coefficient_imaginary * enter_re
        carried_contribution = jnp.einsum(
            "zan,zas->nas", exponent_real, blended_real, precision=largest_value
        ) - jnp.einsum(
            "zan,zas->nas", exponent_imaginary, blended_imaginary, precision=largest_value
        )
        carried_contribution = carried_contribution * alive_dev[:, None, None]
        leave_re = carry_re[:, :, None] * enter_re - carry_im[:, :, None] * enter_im
        leave_im = carry_re[:, :, None] * enter_im + carry_im[:, :, None] * enter_re
        return (carried_contribution, (leave_re, leave_im))

    signal32 = signal.astype(jnp.float32)
    (local_out, local_end), pull_local = jax.vjp(intra, signal32, residues, skip_gain)
    identity = (
        jnp.ones_like(carry_re),
        jnp.zeros_like(carry_re),
        jnp.zeros_like(local_end[0]),
        jnp.zeros_like(local_end[0]),
    )
    entering = carried_in(
        (carry_re, carry_im, local_end[0], local_end[1]), "tm", compose, identity, False
    )
    enter_re, enter_im = (entering[2], entering[3])
    carry_result, pull_carry = jax.vjp(carry_part, residues, enter_re, enter_im)
    long_out = (local_out + carry_result[0]).reshape(rows_dev, channels)
    query32 = query_rows.astype(jnp.float32)
    upstream = grad_out[0].astype(jnp.float32)
    mixed = (query32 * long_out).astype(jnp.bfloat16)
    grad_long = (upstream * query32).reshape(rows_dev, heads_dev, head_width)
    grad_query = (upstream * long_out).astype(jnp.bfloat16)
    zero_state = jnp.zeros_like(enter_re)
    _, adjoint_re, adjoint_im = pull_carry((grad_long, (zero_state, zero_state)))
    leaving = carried_in(
        (carry_re, -carry_im, adjoint_re, adjoint_im), "tm", compose, identity, True
    )
    end_re, end_im = (leaving[2], leaving[3])
    coeff_carry, _, _ = pull_carry((grad_long, (end_re, end_im)))
    grad_signal, coeff_local, skip_local = pull_local((grad_long, (end_re, end_im)))
    grad_value = grad_signal.astype(jnp.bfloat16)
    stacked = jnp.stack([grad_query, grad_value])
    partial_in = jnp.einsum("klc,kdc->ld", stacked, in_proj, preferred_element_type=jnp.float32)
    input_grad = lax.psum_scatter(
        partial_in[None], "tensor", scatter_dimension=2, tiled=True
    ).astype(jnp.bfloat16)
    norm_scale = 1.0 / math.sqrt(rows_dev * lax.axis_size("tm") * lax.axis_size("dp"))
    proj_term = (
        jnp.einsum("ld,klc->kdc", features, stacked, preferred_element_type=jnp.float32)
        * norm_scale
    )
    coeff_term = (coeff_local + coeff_carry) * norm_scale
    skip_term = skip_local * norm_scale
    proj_sum, coeff_sum, skip_sum = lax.psum((proj_term, coeff_term, skip_term), ("tm", "dp"))
    return (mixed[None], input_grad, proj_sum, coeff_sum, skip_sum)


def solution(mesh):
    in_specs = (
        P(("group", "dp"), "tm", "tensor"),
        P(None, None, "tensor"),
        P(None, "tensor"),
        P(None, "tensor"),
        P(None, None, "tensor"),
        P("tensor"),
        P(("group", "dp"), None),
        P(("group", "dp"), "tm", "tensor"),
    )
    out_specs = (
        P(("group", "dp"), "tm", "tensor"),
        P(("group", "dp"), "tm", "tensor"),
        P("group", None, "tensor"),
        P("group", None, "tensor"),
        P(("group", "tensor")),
    )
    return jax.shard_map(shards, mesh=mesh, in_specs=in_specs, out_specs=out_specs, check_vma=False)
```

profile of v0, /device:TPU:0, one launch (start us, length us, event | category | flops | bytes accessed | tf_op | source)
XLA Modules:
  0.0 767.0 jit_solution(7219482252016499978)
XLA Ops:
  13.0 14.9 %all-gather = f32[32,4,1]{2,0,1:T(8,128)S(1)} all-gather(f32[8,4,1]{2,0,1:T(8,128)S(1)} %get-tuple-element.1668), channel_id=2, replica_groups=mesh['group'=2,'tm'=4,'tensor'=2,'dp'=2] {'tm'}, dimensions={0}, use_global_device_ids=true | all-gather | bytes 640 | tf_op jit(solution)/shard_map/all_gather | solution.py:12
  28.0 13.3 %all-gather.1 = f32[32,4,1]{2,0,1:T(8,128)S(1)} all-gather(f32[8,4,1]{2,0,1:T(8,128)S(1)} %get-tuple-element.1667), channel_id=3, replica_groups=mesh['group'=2,'tm'=4,'tensor'=2,'dp'=2] {'tm'}, dimensions={0}, use_global_device_ids=true | all-gather | bytes 640 | tf_op jit(solution)/shard_map/all_gather | solution.py:12
  41.6 13.2 %all-gather.6 = f32[32,4,1]{2,0,1:T(8,128)S(1)} all-gather(f32[8,4,1]{2,0,1:T(8,128)S(1)} %neg.55), channel_id=8, replica_groups=mesh['group'=2,'tm'=4,'tensor'=2,'dp'=2] {'tm'}, dimensions={0}, use_global_device_ids=true | all-gather | bytes 640 | tf_op jit(solution)/shard_map/all_gather | solution.py:12
  79.1 145.3 %while.82 = (s32[]{:T(128)}, f32[8,4,128]{2,0,1:T(8,128)S(1)}, f32[8,4,128]{2,0,1:T(8,128)S(1)}, f32[6,128,4,128]{3,1,0,2:T(8,128)}, f32[6,8,4,128]{3,1,2,0:T(8,...) while((s32[]{:T(128)}, f32[8,4,128]{2,0,1:T(8,128)S(1)}, ...), condition=%wide.region_4.5_spmd.clone.clone, body=%wide.region_3.4_spmd.clone.clone.sunk | while | flops 1623294208 | bytes 7542485 | solution.py:124
  82.1 10.2 %multiply_reduce_fusion.11 = (f32[4,128,128]{1,2,0:T(8,128)S(1)}, f32[8,4,128,128]{3,2,0,1:T(8,128)S(1)}) fusion(f32[4,128,8]{1,2,0:T(8,128)S(1)} %copy.360, f32[8,4,128]{2,0,1:T(8,128)S(1)} %get-tuple-element.2158, f32[8,4,128]{2,0,1:T(8,128)S(1)} %bitcast.427, f32[8,4,128]{2,0,1:T(8,128)S(1)} %get-tuple-element.2159, ...), kind=kOutput, calls=%fused_computation.88.clone.1 | convolution fusion | flops 811532288 | bytes 2851584 | tf_op jit(solution)/shard_map/jvp()/while/body/eval_jaxpr/mhts,shd->mhtd/dot_general | solution.py:97
  92.3 10.3 %multiply_reduce_fusion.10 = (f32[4,128,128]{1,2,0:T(8,128)S(1)}, f32[8,4,128,128]{3,2,0,1:T(8,128)S(1)}) fusion(f32[4,128,8]{1,2,0:T(8,128)S(1)} %copy.359, f32[8,4,128]{2,0,1:T(8,128)S(1)} %get-tuple-element.2159, f32[8,4,128]{2,0,1:T(8,128)S(1)} %bitcast.428, f32[8,4,128]{2,0,1:T(8,128)S(1)} %get-tuple-element.2158, ...), kind=kOutput, calls=%fused_computation.89.clone.1 | convolution fusion | flops 811532288 | bytes 2851584 | tf_op jit(solution)/shard_map/jvp()/while/body/eval_jaxpr/mhts,shd->mhtd/dot_general | solution.py:94
  106.2 10.2 %multiply_reduce_fusion.11 = (f32[4,128,128]{1,2,0:T(8,128)S(1)}, f32[8,4,128,128]{3,2,0,1:T(8,128)S(1)}) fusion(f32[4,128,8]{1,2,0:T(8,128)S(1)} %copy.360, f32[8,4,128]{2,0,1:T(8,128)S(1)} %get-tuple-element.2158, f32[8,4,128]{2,0,1:T(8,128)S(1)} %bitcast.427, f32[8,4,128]{2,0,1:T(8,128)S(1)} %get-tuple-element.2159, ...), kind=kOutput, calls=%fused_computation.88.clone.1 | convolution fusion | flops 811532288 | bytes 2851584 | tf_op jit(solution)/shard_map/jvp()/while/body/eval_jaxpr/mhts,shd->mhtd/dot_general | solution.py:97
  116.4 10.3 %multiply_reduce_fusion.10 = (f32[4,128,128]{1,2,0:T(8,128)S(1)}, f32[8,4,128,128]{3,2,0,1:T(8,128)S(1)}) fusion(f32[4,128,8]{1,2,0:T(8,128)S(1)} %copy.359, f32[8,4,128]{2,0,1:T(8,128)S(1)} %get-tuple-element.2159, f32[8,4,128]{2,0,1:T(8,128)S(1)} %bitcast.428, f32[8,4,128]{2,0,1:T(8,128)S(1)} %get-tuple-element.2158, ...), kind=kOutput, calls=%fused_computation.89.clone.1 | convolution fusion | flops 811532288 | bytes 2851584 | tf_op jit(solution)/shard_map/jvp()/while/body/eval_jaxpr/mhts,shd->mhtd/dot_general | solution.py:94
  130.4 10.2 %multiply_reduce_fusion.11 = (f32[4,128,128]{1,2,0:T(8,128)S(1)}, f32[8,4,128,128]{3,2,0,1:T(8,128)S(1)}) fusion(f32[4,128,8]{1,2,0:T(8,128)S(1)} %copy.360, f32[8,4,128]{2,0,1:T(8,128)S(1)} %get-tuple-element.2158, f32[8,4,128]{2,0,1:T(8,128)S(1)} %bitcast.427, f32[8,4,128]{2,0,1:T(8,128)S(1)} %get-tuple-element.2159, ...), kind=kOutput, calls=%fused_computation.88.clone.1 | convolution fusion | flops 811532288 | bytes 2851584 | tf_op jit(solution)/shard_map/jvp()/while/body/eval_jaxpr/mhts,shd->mhtd/dot_general | solution.py:97
  140.6 10.3 %multiply_reduce_fusion.10 = (f32[4,128,128]{1,2,0:T(8,128)S(1)}, f32[8,4,128,128]{3,2,0,1:T(8,128)S(1)}) fusion(f32[4,128,8]{1,2,0:T(8,128)S(1)} %copy.359, f32[8,4,128]{2,0,1:T(8,128)S(1)} %get-tuple-element.2159, f32[8,4,128]{2,0,1:T(8,128)S(1)} %bitcast.428, f32[8,4,128]{2,0,1:T(8,128)S(1)} %get-tuple-element.2158, ...), kind=kOutput, calls=%fused_computation.89.clone.1 | convolution fusion | flops 811532288 | bytes 2851584 | tf_op jit(solution)/shard_map/jvp()/while/body/eval_jaxpr/mhts,shd->mhtd/dot_general | solution.py:94
  154.5 10.2 %multiply_reduce_fusion.11 = (f32[4,128,128]{1,2,0:T(8,128)S(1)}, f32[8,4,128,128]{3,2,0,1:T(8,128)S(1)}) fusion(f32[4,128,8]{1,2,0:T(8,128)S(1)} %copy.360, f32[8,4,128]{2,0,1:T(8,128)S(1)} %get-tuple-element.2158, f32[8,4,128]{2,0,1:T(8,128)S(1)} %bitcast.427, f32[8,4,128]{2,0,1:T(8,128)S(1)} %get-tuple-element.2159, ...), kind=kOutput, calls=%fused_computation.88.clone.1 | convolution fusion | flops 811532288 | bytes 2851584 | tf_op jit(solution)/shard_map/jvp()/while/body/eval_jaxpr/mhts,shd->mhtd/dot_general | solution.py:97
  164.7 10.3 %multiply_reduce_fusion.10 = (f32[4,128,128]{1,2,0:T(8,128)S(1)}, f32[8,4,128,128]{3,2,0,1:T(8,128)S(1)}) fusion(f32[4,128,8]{1,2,0:T(8,128)S(1)} %copy.359, f32[8,4,128]{2,0,1:T(8,128)S(1)} %get-tuple-element.2159, f32[8,4,128]{2,0,1:T(8,128)S(1)} %bitcast.428, f32[8,4,128]{2,0,1:T(8,128)S(1)} %get-tuple-element.2158, ...), kind=kOutput, calls=%fused_computation.89.clone.1 | convolution fusion | flops 811532288 | bytes 2851584 | tf_op jit(solution)/shard_map/jvp()/while/body/eval_jaxpr/mhts,shd->mhtd/dot_general | solution.py:94
  178.6 10.2 %multiply_reduce_fusion.11 = (f32[4,128,128]{1,2,0:T(8,128)S(1)}, f32[8,4,128,128]{3,2,0,1:T(8,128)S(1)}) fusion(f32[4,128,8]{1,2,0:T(8,128)S(1)} %copy.360, f32[8,4,128]{2,0,1:T(8,128)S(1)} %get-tuple-element.2158, f32[8,4,128]{2,0,1:T(8,128)S(1)} %bitcast.427, f32[8,4,128]{2,0,1:T(8,128)S(1)} %get-tuple-element.2159, ...), kind=kOutput, calls=%fused_computation.88.clone.1 | convolution fusion | flops 811532288 | bytes 2851584 | tf_op jit(solution)/shard_map/jvp()/while/body/eval_jaxpr/mhts,shd->mhtd/dot_general | solution.py:97
  188.8 10.3 %multiply_reduce_fusion.10 = (f32[4,128,128]{1,2,0:T(8,128)S(1)}, f32[8,4,128,128]{3,2,0,1:T(8,128)S(1)}) fusion(f32[4,128,8]{1,2,0:T(8,128)S(1)} %copy.359, f32[8,4,128]{2,0,1:T(8,128)S(1)} %get-tuple-element.2159, f32[8,4,128]{2,0,1:T(8,128)S(1)} %bitcast.428, f32[8,4,128]{2,0,1:T(8,128)S(1)} %get-tuple-element.2158, ...), kind=kOutput, calls=%fused_computation.89.clone.1 | convolution fusion | flops 811532288 | bytes 2851584 | tf_op jit(solution)/shard_map/jvp()/while/body/eval_jaxpr/mhts,shd->mhtd/dot_general | solution.py:94
  202.7 10.2 %multiply_reduce_fusion.11 = (f32[4,128,128]{1,2,0:T(8,128)S(1)}, f32[8,4,128,128]{3,2,0,1:T(8,128)S(1)}) fusion(f32[4,128,8]{1,2,0:T(8,128)S(1)} %copy.360, f32[8,4,128]{2,0,1:T(8,128)S(1)} %get-tuple-element.2158, f32[8,4,128]{2,0,1:T(8,128)S(1)} %bitcast.427, f32[8,4,128]{2,0,1:T(8,128)S(1)} %get-tuple-element.2159, ...), kind=kOutput, calls=%fused_computation.88.clone.1 | convolution fusion | flops 811532288 | bytes 2851584 | tf_op jit(solution)/shard_map/jvp()/while/body/eval_jaxpr/mhts,shd->mhtd/dot_general | solution.py:97
  212.9 10.3 %multiply_reduce_fusion.10 = (f32[4,128,128]{1,2,0:T(8,128)S(1)}, f32[8,4,128,128]{3,2,0,1:T(8,128)S(1)}) fusion(f32[4,128,8]{1,2,0:T(8,128)S(1)} %copy.359, f32[8,4,128]{2,0,1:T(8,128)S(1)} %get-tuple-element.2159, f32[8,4,128]{2,0,1:T(8,128)S(1)} %bitcast.428, f32[8,4,128]{2,0,1:T(8,128)S(1)} %get-tuple-element.2158, ...), kind=kOutput, calls=%fused_computation.89.clone.1 | convolution fusion | flops 811532288 | bytes 2851584 | tf_op jit(solution)/shard_map/jvp()/while/body/eval_jaxpr/mhts,shd->mhtd/dot_general | solution.py:94
  227.4 13.2 %all-gather.2 = f32[32,4,128]{2,0,1:T(8,128)S(1)} all-gather(f32[8,4,128]{2,0,1:T(8,128)S(1)} %get-tuple-element.821), channel_id=4, replica_groups=mesh['group'=2,'tm'=4,'tensor'=2,'dp'=2] {'tm'}, dimensions={0}, use_global_device_ids=true | all-gather | bytes 81920 | tf_op jit(solution)/shard_map/all_gather | solution.py:12
  240.6 13.2 %all-gather.3 = f32[32,4,128]{2,0,1:T(8,128)S(1)} all-gather(f32[8,4,128]{2,0,1:T(8,128)S(1)} %get-tuple-element.822), channel_id=5, replica_groups=mesh['group'=2,'tm'=4,'tensor'=2,'dp'=2] {'tm'}, dimensions={0}, use_global_device_ids=true | all-gather | bytes 81920 | tf_op jit(solution)/shard_map/all_gather | solution.py:12
  260.5 13.2 %all-gather.4 = f32[32,4,128]{2,0,1:T(8,128)S(1)} all-gather(f32[8,4,128]{2,0,1:T(8,128)S(1)} %get-tuple-element.1700), channel_id=6, replica_groups=mesh['group'=2,'tm'=4,'tensor'=2,'dp'=2] {'tm'}, dimensions={0}, use_global_device_ids=true | all-gather | bytes 81920 | tf_op jit(solution)/shard_map/all_gather | solution.py:12
  273.7 13.2 %all-gather.5 = f32[32,4,128]{2,0,1:T(8,128)S(1)} all-gather(f32[8,4,128]{2,0,1:T(8,128)S(1)} %get-tuple-element.1664), channel_id=7, replica_groups=mesh['group'=2,'tm'=4,'tensor'=2,'dp'=2] {'tm'}, dimensions={0}, use_global_device_ids=true | all-gather | bytes 81920 | tf_op jit(solution)/shard_map/all_gather | solution.py:12
  290.1 313.4 %while.83 = (s32[]{:T(128)}, f32[4,128]{1,0:T(4,128)S(1)}, f32[8,4,128]{2,1,0:T(4,128)}, f32[8,4,128]{2,1,0:T(4,128)}, f32[8,4,128]{2,0,1:T(8,128)}, /*index=5*/...) while((s32[]{:T(128)}, f32[4,128]{1,0:T(4,128)S(1)}, ...), condition=%wide.region_15.16_spmd.clone.clone.clone, body=%wide.region_9.15_spmd.clone.clone.clone.sunk | while | flops 3254166272 | bytes 45512152 | solution.py:124
  290.3 10.1 %fusion.192 = (f32[8,4,128,128]{3,2,0,1:T(8,128)}, f32[8,4,128,128]{3,2,0,1:T(8,128)}) fusion(f32[8,4]{0,1:T(4,128)S(1)} %get-tuple-element.2326, f32[128,128]{1,0:T(8,128)} %get-tuple-element.2325, f32[8,4]{0,1:T(4,128)S(1)} %get-tuple-element.2323, pred[128,128]{1,0:T(8,128)(4,1)S(1)} %get-tuple-element.2324), kind=kLoop, calls=%fused_computation.23.clone.1 | loop fusion | flops 2621440 | bytes 4276480 | tf_op jit(solution)/shard_map/mul | solution.py:57
  307.0 4.1 bitcast_add_fusion.17
  311.1 4.5 fusion.194
  315.7 4.2 bitcast_add_fusion.18
  320.0 4.5 fusion.195
  328.7 6.1 multiply_reduce_fusion.12
  338.8 3.6 fusion.197
  342.5 10.1 %fusion.192 = (f32[8,4,128,128]{3,2,0,1:T(8,128)}, f32[8,4,128,128]{3,2,0,1:T(8,128)}) fusion(f32[8,4]{0,1:T(4,128)S(1)} %get-tuple-element.2326, f32[128,128]{1,0:T(8,128)} %get-tuple-element.2325, f32[8,4]{0,1:T(4,128)S(1)} %get-tuple-element.2323, pred[128,128]{1,0:T(8,128)(4,1)S(1)} %get-tuple-element.2324), kind=kLoop, calls=%fused_computation.23.clone.1 | loop fusion | flops 2621440 | bytes 4276480 | tf_op jit(solution)/shard_map/mul | solution.py:57
  359.2 4.1 bitcast_add_fusion.17
  363.3 4.5 fusion.194
  367.9 4.2 bitcast_add_fusion.18
  372.1 4.5 fusion.195
  380.9 6.1 multiply_reduce_fusion.12
  394.7 10.1 %fusion.192 = (f32[8,4,128,128]{3,2,0,1:T(8,128)}, f32[8,4,128,128]{3,2,0,1:T(8,128)}) fusion(f32[8,4]{0,1:T(4,128)S(1)} %get-tuple-element.2326, f32[128,128]{1,0:T(8,128)} %get-tuple-element.2325, f32[8,4]{0,1:T(4,128)S(1)} %get-tuple-element.2323, pred[128,128]{1,0:T(8,128)(4,1)S(1)} %get-tuple-element.2324), kind=kLoop, calls=%fused_computation.23.clone.1 | loop fusion | flops 2621440 | bytes 4276480 | tf_op jit(solution)/shard_map/mul | solution.py:57
  411.3 4.1 bitcast_add_fusion.17
  415.5 4.5 fusion.194
  420.1 4.2 bitcast_add_fusion.18
  424.3 4.5 fusion.195
  433.1 6.1 multiply_reduce_fusion.12
  446.9 10.1 %fusion.192 = (f32[8,4,128,128]{3,2,0,1:T(8,128)}, f32[8,4,128,128]{3,2,0,1:T(8,128)}) fusion(f32[8,4]{0,1:T(4,128)S(1)} %get-tuple-element.2326, f32[128,128]{1,0:T(8,128)} %get-tuple-element.2325, f32[8,4]{0,1:T(4,128)S(1)} %get-tuple-element.2323, pred[128,128]{1,0:T(8,128)(4,1)S(1)} %get-tuple-element.2324), kind=kLoop, calls=%fused_computation.23.clone.1 | loop fusion | flops 2621440 | bytes 4276480 | tf_op jit(solution)/shard_map/mul | solution.py:57
  463.5 4.1 bitcast_add_fusion.17
  467.6 4.5 fusion.194
  472.2 4.2 bitcast_add_fusion.18
  476.5 4.5 fusion.195
  485.3 6.1 multiply_reduce_fusion.12
  499.1 10.1 %fusion.192 = (f32[8,4,128,128]{3,2,0,1:T(8,128)}, f32[8,4,128,128]{3,2,0,1:T(8,128)}) fusion(f32[8,4]{0,1:T(4,128)S(1)} %get-tuple-element.2326, f32[128,128]{1,0:T(8,128)} %get-tuple-element.2325, f32[8,4]{0,1:T(4,128)S(1)} %get-tuple-element.2323, pred[128,128]{1,0:T(8,128)(4,1)S(1)} %get-tuple-element.2324), kind=kLoop, calls=%fused_computation.23.clone.1 | loop fusion | flops 2621440 | bytes 4276480 | tf_op jit(solution)/shard_map/mul | solution.py:57
  515.7 4.1 bitcast_add_fusion.17
  519.8 4.5 fusion.194
  524.4 4.2 bitcast_add_fusion.18
  528.7 4.5 fusion.195
  537.4 6.1 multiply_reduce_fusion.12
  551.3 10.1 %fusion.192 = (f32[8,4,128,128]{3,2,0,1:T(8,128)}, f32[8,4,128,128]{3,2,0,1:T(8,128)}) fusion(f32[8,4]{0,1:T(4,128)S(1)} %get-tuple-element.2326, f32[128,128]{1,0:T(8,128)} %get-tuple-element.2325, f32[8,4]{0,1:T(4,128)S(1)} %get-tuple-element.2323, pred[128,128]{1,0:T(8,128)(4,1)S(1)} %get-tuple-element.2324), kind=kLoop, calls=%fused_computation.23.clone.1 | loop fusion | flops 2621440 | bytes 4276480 | tf_op jit(solution)/shard_map/mul | solution.py:57
  567.9 4.1 bitcast_add_fusion.17
  572.0 4.5 fusion.194
  576.6 4.2 bitcast_add_fusion.18
  580.9 4.5 fusion.195
  589.6 6.1 multiply_reduce_fusion.12
  607.7 5.7 multiply_bitcast_fusion
  614.5 4.7 convolution_bitcast_fusion
  621.7 29.1 %all-reduce.6 = (f32[2,8,512]{2,1,0:T(8,128)}, f32[512]{0:T(512)}) all-reduce(f32[2,8,512]{2,1,0:T(8,128)S(1)} %add_multiply_fusion, f32[512]{0:T(512)S(1)} %multiply_bitcast_fusion.3), channel_id=1, replica_groups=mesh['group'=2,'tm'=4,'tensor'=2,'dp'=2] {'tm','dp'}, use_global_device_ids=true, to_apply=%region_18.19 | all-reduce | flops 8704 | bytes 69632 | tf_op jit(solution)/shard_map/psum | solution.py:183
  650.8 61.4 %all-reduce.9.cloned.1.call-done = f32[2,1024,512]{1,2,0:T(8,128)} async-done(((f32[2,1024,512]{1,2,0:T(8,128)}), f32[2,1024,512]{1,2,0:T(8,128)}) %all-reduce.9.cloned.1.call-update) | async-done | bytes 4194320 | tf_op jit(solution)/shard_map/psum | solution.py:183
  712.2 5.4 copy.231
  717.5 40.3 %reduce-scatter.2.cloned.1.call-done = f32[1,768,512]{2,1,0:T(8,128)} async-done(((f32[1,768,1024]{2,1,0:T(8,128)}), f32[1,768,512]{2,1,0:T(8,128)}) %reduce-scatter.2.cloned.1.call-update) | async-done | bytes 1572880 | tf_op jit(solution)/shard_map/reduce_scatter | solution.py:173
  (647 shorter events, 181.7 us)
Async XLA Ops:
  7.2 48.8 %copy-start = (bf16[2,1024,512]{2,1,0:T(8,128)(2,1)S(1)}, bf16[2,1024,512]{2,1,0:T(8,128)(2,1)}, u32[]{:S(2)}) copy-start(bf16[2,1024,512]{2,1,0:T(8,128)(2,1)} %param.17) | copy-start | bytes 6291460
  7.2 48.7 %all-gather.9.cloned.1.call-start = ((), (), s32[]{:S(2)}) async-start(), calls=%async_computation.1 | async-start | bytes 2359296 | tf_op jit(solution)/shard_map/all_gather | solution.py:45
  7.9 704.2 %all-reduce.9.cloned.1.call-start = ((), (), s32[]{:S(2)}) async-start(), calls=%async_computation.3 | async-start | bytes 8388608 | tf_op jit(solution)/shard_map/psum | solution.py:183
  11.7 248.1 %copy-start.38 = (f32[8,4]{0,1:T(4,128)}, f32[8,4]{0,1:T(4,128)S(1)}, u32[]{:S(2)}) copy-start(f32[8,4]{0,1:T(4,128)S(1)} %get-tuple-element.1705) | copy-start | bytes 388
  259.8 30.4 %copy-start.31 = (f32[4,128]{1,0:T(4,128)S(1)}, f32[4,128]{1,0:T(4,128)}, u32[]{:S(2)}) copy-start(f32[4,128]{1,0:T(4,128)} %custom-call.4) | copy-start | bytes 6148
  290.3 10.2 %copy-start.11 = (pred[128,128]{1,0:T(8,128)(4,1)}, pred[128,128]{1,0:T(8,128)(4,1)S(1)}, u32[]{:S(2)}) copy-start(pred[128,128]{1,0:T(8,128)(4,1)S(1)} %get-tuple-element.2324) | copy-start | bytes 49156 | tf_op jit(solution)/shard_map/transpose(jvp())/while
  290.3 10.1 %copy-start.21 = (f32[8,4]{0,1:T(4,128)}, f32[8,4]{0,1:T(4,128)S(1)}, u32[]{:S(2)}) copy-start(f32[8,4]{0,1:T(4,128)S(1)} %get-tuple-element.2323) | copy-start | bytes 388 | tf_op jit(solution)/shard_map/transpose(jvp())/while
  290.3 10.1 %copy-start.24 = (f32[8,4]{0,1:T(4,128)}, f32[8,4]{0,1:T(4,128)S(1)}, u32[]{:S(2)}) copy-start(f32[8,4]{0,1:T(4,128)S(1)} %get-tuple-element.2326) | copy-start | bytes 388 | tf_op jit(solution)/shard_map/transpose(jvp())/while
  290.3 10.1 %copy-start.27 = (f32[4,128]{1,0:T(4,128)}, f32[4,128]{1,0:T(4,128)S(1)}, u32[]{:S(2)}) copy-start(f32[4,128]{1,0:T(4,128)S(1)} %get-tuple-element.2137) | copy-start | bytes 6148 | tf_op jit(solution)/shard_map/transpose(jvp())/while
  290.3 12.7 %copy-start.40 = (s32[6,128]{1,0:T(8,128)}, s32[6,128]{1,0:T(8,128)S(1)}, u32[]{:S(2)}) copy-start(s32[6,128]{1,0:T(8,128)S(1)} %get-tuple-element.2315) | copy-start | bytes 9220 | tf_op jit(solution)/shard_map/transpose(jvp())/while
  290.3 12.7 %copy-start.45 = (s32[6]{0:T(128)}, s32[6]{0:T(128)S(1)}, u32[]{:S(2)}) copy-start(s32[6]{0:T(128)S(1)} %get-tuple-element.2316) | copy-start | bytes 76 | tf_op jit(solution)/shard_map/transpose(jvp())/while
  320.0 6.7 copy-start.13
  328.7 7.3 copy-start.1
  328.7 7.3 copy-start.2
  328.7 7.3 copy-start.28
  342.5 10.2 %copy-start.11 = (pred[128,128]{1,0:T(8,128)(4,1)}, pred[128,128]{1,0:T(8,128)(4,1)S(1)}, u32[]{:S(2)}) copy-start(pred[128,128]{1,0:T(8,128)(4,1)S(1)} %get-tuple-element.2324) | copy-start | bytes 49156 | tf_op jit(solution)/shard_map/transpose(jvp())/while
  342.5 10.1 %copy-start.21 = (f32[8,4]{0,1:T(4,128)}, f32[8,4]{0,1:T(4,128)S(1)}, u32[]{:S(2)}) copy-start(f32[8,4]{0,1:T(4,128)S(1)} %get-tuple-element.2323) | copy-start | bytes 388 | tf_op jit(solution)/shard_map/transpose(jvp())/while
  342.5 10.1 %copy-start.24 = (f32[8,4]{0,1:T(4,128)}, f32[8,4]{0,1:T(4,128)S(1)}, u32[]{:S(2)}) copy-start(f32[8,4]{0,1:T(4,128)S(1)} %get-tuple-element.2326) | copy-start | bytes 388 | tf_op jit(solution)/shard_map/transpose(jvp())/while
  342.5 10.1 %copy-start.27 = (f32[4,128]{1,0:T(4,128)}, f32[4,128]{1,0:T(4,128)S(1)}, u32[]{:S(2)}) copy-start(f32[4,128]{1,0:T(4,128)S(1)} %get-tuple-element.2137) | copy-start | bytes 6148 | tf_op jit(solution)/shard_map/transpose(jvp())/while
  342.5 12.7 %copy-start.40 = (s32[6,128]{1,0:T(8,128)}, s32[6,128]{1,0:T(8,128)S(1)}, u32[]{:S(2)}) copy-start(s32[6,128]{1,0:T(8,128)S(1)} %get-tuple-element.2315) | copy-start | bytes 9220 | tf_op jit(solution)/shard_map/transpose(jvp())/while
  342.5 12.7 %copy-start.45 = (s32[6]{0:T(128)}, s32[6]{0:T(128)S(1)}, u32[]{:S(2)}) copy-start(s32[6]{0:T(128)S(1)} %get-tuple-element.2316) | copy-start | bytes 76 | tf_op jit(solution)/shard_map/transpose(jvp())/while
  380.9 7.3 copy-start.1
  380.9 7.3 copy-start.2
  380.9 7.3 copy-start.28
  394.7 10.2 %copy-start.11 = (pred[128,128]{1,0:T(8,128)(4,1)}, pred[128,128]{1,0:T(8,128)(4,1)S(1)}, u32[]{:S(2)}) copy-start(pred[128,128]{1,0:T(8,128)(4,1)S(1)} %get-tuple-element.2324) | copy-start | bytes 49156 | tf_op jit(solution)/shard_map/transpose(jvp())/while
  394.7 10.1 %copy-start.21 = (f32[8,4]{0,1:T(4,128)}, f32[8,4]{0,1:T(4,128)S(1)}, u32[]{:S(2)}) copy-start(f32[8,4]{0,1:T(4,128)S(1)} %get-tuple-element.2323) | copy-start | bytes 388 | tf_op jit(solution)/shard_map/transpose(jvp())/while
  394.7 10.1 %copy-start.24 = (f32[8,4]{0,1:T(4,128)}, f32[8,4]{0,1:T(4,128)S(1)}, u32[]{:S(2)}) copy-start(f32[8,4]{0,1:T(4,128)S(1)} %get-tuple-element.2326) | copy-start | bytes 388 | tf_op jit(solution)/shard_map/transpose(jvp())/while
  394.7 10.1 %copy-start.27 = (f32[4,128]{1,0:T(4,128)}, f32[4,128]{1,0:T(4,128)S(1)}, u32[]{:S(2)}) copy-start(f32[4,128]{1,0:T(4,128)S(1)} %get-tuple-element.2137) | copy-start | bytes 6148 | tf_op jit(solution)/shard_map/transpose(jvp())/while
  394.7 12.7 %copy-start.40 = (s32[6,128]{1,0:T(8,128)}, s32[6,128]{1,0:T(8,128)S(1)}, u32[]{:S(2)}) copy-start(s32[6,128]{1,0:T(8,128)S(1)} %get-tuple-element.2315) | copy-start | bytes 9220 | tf_op jit(solution)/shard_map/transpose(jvp())/while
  394.7 12.7 %copy-start.45 = (s32[6]{0:T(128)}, s32[6]{0:T(128)S(1)}, u32[]{:S(2)}) copy-start(s32[6]{0:T(128)S(1)} %get-tuple-element.2316) | copy-start | bytes 76 | tf_op jit(solution)/shard_map/transpose(jvp())/while
  433.1 7.3 copy-start.1
  433.1 7.3 copy-start.2
  433.1 7.3 copy-start.28
  446.8 10.2 %copy-start.11 = (pred[128,128]{1,0:T(8,128)(4,1)}, pred[128,128]{1,0:T(8,128)(4,1)S(1)}, u32[]{:S(2)}) copy-start(pred[128,128]{1,0:T(8,128)(4,1)S(1)} %get-tuple-element.2324) | copy-start | bytes 49156 | tf_op jit(solution)/shard_map/transpose(jvp())/while
  446.8 10.1 %copy-start.21 = (f32[8,4]{0,1:T(4,128)}, f32[8,4]{0,1:T(4,128)S(1)}, u32[]{:S(2)}) copy-start(f32[8,4]{0,1:T(4,128)S(1)} %get-tuple-element.2323) | copy-start | bytes 388 | tf_op jit(solution)/shard_map/transpose(jvp())/while
  446.9 10.1 %copy-start.24 = (f32[8,4]{0,1:T(4,128)}, f32[8,4]{0,1:T(4,128)S(1)}, u32[]{:S(2)}) copy-start(f32[8,4]{0,1:T(4,128)S(1)} %get-tuple-element.2326) | copy-start | bytes 388 | tf_op jit(solution)/shard_map/transpose(jvp())/while
  446.9 10.1 %copy-start.27 = (f32[4,128]{1,0:T(4,128)}, f32[4,128]{1,0:T(4,128)S(1)}, u32[]{:S(2)}) copy-start(f32[4,128]{1,0:T(4,128)S(1)} %get-tuple-element.2137) | copy-start | bytes 6148 | tf_op jit(solution)/shard_map/transpose(jvp())/while
  446.9 12.7 %copy-start.40 = (s32[6,128]{1,0:T(8,128)}, s32[6,128]{1,0:T(8,128)S(1)}, u32[]{:S(2)}) copy-start(s32[6,128]{1,0:T(8,128)S(1)} %get-tuple-element.2315) | copy-start | bytes 9220 | tf_op jit(solution)/shard_map/transpose(jvp())/while
  446.9 12.7 %copy-start.45 = (s32[6]{0:T(128)}, s32[6]{0:T(128)S(1)}, u32[]{:S(2)}) copy-start(s32[6]{0:T(128)S(1)} %get-tuple-element.2316) | copy-start | bytes 76 | tf_op jit(solution)/shard_map/transpose(jvp())/while
  476.5 6.7 copy-start.13
  485.2 7.3 copy-start.1
  485.2 7.3 copy-start.2
  485.3 7.3 copy-start.28
  499.0 10.2 %copy-start.11 = (pred[128,128]{1,0:T(8,128)(4,1)}, pred[128,128]{1,0:T(8,128)(4,1)S(1)}, u32[]{:S(2)}) copy-start(pred[128,128]{1,0:T(8,128)(4,1)S(1)} %get-tuple-element.2324) | copy-start | bytes 49156 | tf_op jit(solution)/shard_map/transpose(jvp())/while
  499.0 10.1 %copy-start.21 = (f32[8,4]{0,1:T(4,128)}, f32[8,4]{0,1:T(4,128)S(1)}, u32[]{:S(2)}) copy-start(f32[8,4]{0,1:T(4,128)S(1)} %get-tuple-element.2323) | copy-start | bytes 388 | tf_op jit(solution)/shard_map/transpose(jvp())/while
  499.0 10.1 %copy-start.24 = (f32[8,4]{0,1:T(4,128)}, f32[8,4]{0,1:T(4,128)S(1)}, u32[]{:S(2)}) copy-start(f32[8,4]{0,1:T(4,128)S(1)} %get-tuple-element.2326) | copy-start | bytes 388 | tf_op jit(solution)/shard_map/transpose(jvp())/while
  499.0 10.1 %copy-start.27 = (f32[4,128]{1,0:T(4,128)}, f32[4,128]{1,0:T(4,128)S(1)}, u32[]{:S(2)}) copy-start(f32[4,128]{1,0:T(4,128)S(1)} %get-tuple-element.2137) | copy-start | bytes 6148 | tf_op jit(solution)/shard_map/transpose(jvp())/while
  499.1 12.7 %copy-start.40 = (s32[6,128]{1,0:T(8,128)}, s32[6,128]{1,0:T(8,128)S(1)}, u32[]{:S(2)}) copy-start(s32[6,128]{1,0:T(8,128)S(1)} %get-tuple-element.2315) | copy-start | bytes 9220 | tf_op jit(solution)/shard_map/transpose(jvp())/while
  499.1 12.7 %copy-start.45 = (s32[6]{0:T(128)}, s32[6]{0:T(128)S(1)}, u32[]{:S(2)}) copy-start(s32[6]{0:T(128)S(1)} %get-tuple-element.2316) | copy-start | bytes 76 | tf_op jit(solution)/shard_map/transpose(jvp())/while
  528.7 6.7 copy-start.13
  537.4 7.3 copy-start.1
  537.4 7.3 copy-start.2
  537.4 7.3 copy-start.28
  551.2 10.2 %copy-start.11 = (pred[128,128]{1,0:T(8,128)(4,1)}, pred[128,128]{1,0:T(8,128)(4,1)S(1)}, u32[]{:S(2)}) copy-start(pred[128,128]{1,0:T(8,128)(4,1)S(1)} %get-tuple-element.2324) | copy-start | bytes 49156 | tf_op jit(solution)/shard_map/transpose(jvp())/while
  551.2 10.1 %copy-start.21 = (f32[8,4]{0,1:T(4,128)}, f32[8,4]{0,1:T(4,128)S(1)}, u32[]{:S(2)}) copy-start(f32[8,4]{0,1:T(4,128)S(1)} %get-tuple-element.2323) | copy-start | bytes 388 | tf_op jit(solution)/shard_map/transpose(jvp())/while
  551.2 10.1 %copy-start.24 = (f32[8,4]{0,1:T(4,128)}, f32[8,4]{0,1:T(4,128)S(1)}, u32[]{:S(2)}) copy-start(f32[8,4]{0,1:T(4,128)S(1)} %get-tuple-element.2326) | copy-start | bytes 388 | tf_op jit(solution)/shard_map/transpose(jvp())/while
  551.2 10.1 %copy-start.27 = (f32[4,128]{1,0:T(4,128)}, f32[4,128]{1,0:T(4,128)S(1)}, u32[]{:S(2)}) copy-start(f32[4,128]{1,0:T(4,128)S(1)} %get-tuple-element.2137) | copy-start | bytes 6148 | tf_op jit(solution)/shard_map/transpose(jvp())/while
  551.2 12.7 %copy-start.40 = (s32[6,128]{1,0:T(8,128)}, s32[6,128]{1,0:T(8,128)S(1)}, u32[]{:S(2)}) copy-start(s32[6,128]{1,0:T(8,128)S(1)} %get-tuple-element.2315) | copy-start | bytes 9220 | tf_op jit(solution)/shard_map/transpose(jvp())/while
  551.2 12.7 %copy-start.45 = (s32[6]{0:T(128)}, s32[6]{0:T(128)S(1)}, u32[]{:S(2)}) copy-start(s32[6]{0:T(128)S(1)} %get-tuple-element.2316) | copy-start | bytes 76 | tf_op jit(solution)/shard_map/transpose(jvp())/while
  580.9 6.7 copy-start.13
  589.6 7.3 copy-start.1
  589.6 7.3 copy-start.2
  589.6 7.3 copy-start.28
  613.4 144.4 %reduce-scatter.2.cloned.1.call-start = ((), (), s32[]{:S(2)}) async-start(), calls=%async_computation.2 | async-start | bytes 4718592 | tf_op jit(solution)/shard_map/reduce_scatter | solution.py:173
  (121 other events, 415.1 us)
Sparse Core Ops, SparseCore 0:
  9.6 29.8 all-gather.8
  613.5 98.6 all-reduce.8
  714.4 43.3 reduce-scatter.1
where the time goes:
time: 777 us; the launch traced here: 767 us
  matrix products  288 us (37%)
  other arithmetic  130 us (17%)
  blocking collectives  123 us (16%)
  local copies, waits for them, and re-layouts  104 us (13%)
  waiting for transfers between devices  102 us (13%)
  between operations  15.1 us (2%)
    dot_general x18, matrix products, block_step(): jnp.einsum('mhts,shd->mhtd', kern_re * same_clip, block_in, precision=lar...  108 us
    dot_general x18, matrix products, block_step(): jnp.einsum('mhts,shd->mhtd', kern_im * same_clip, block_in, precision=lar...  102 us
    all_gather x7, blocking collectives, carried_in(): pieces = jax.tree.map(lambda part: lax.all_gather(part, axis), value)  94.2 us
    psum x1, waiting for transfers between devices, shards(): lax.psum((proj_term, coeff_term, skip_term), ('tm', 'dp'))  61.4 us
    mul x6, other arithmetic, shards(): kern_im = damping * jnp.sin(angles[:, :, None, None] * lag_steps)  60.6 us
    reduce_scatter x1, waiting for transfers between devices, shards(): lax.psum_scatter(partial_in[None], 'tensor', scatter_dimension=2, tiled=T...  40.3 us
    reduce_sum x6, other arithmetic, block_step(): block_re[..., None] * state_im[:, :, None, :]  36.6 us
    dynamic_slice x36, local copies, waits for them, and re-layouts, intra(): lax.scan(jax.checkpoint(block_step), (initial, initial), (blocks_in, seg_...  30.9 us
  transfers between devices with their start and end apart: 3, of which 2 were waited for; matrix products, arithmetic and copies ran while one was open for 2% of the time, Pallas kernels for 0%

commit v1 on v0

--- a/solution.py
+++ b/solution.py
@@ -3,6 +3,7 @@
 import jax.numpy as jnp
 from jax import lax
 from jax.sharding import PartitionSpec as P
+from jax.lax import psum
 
 BLOCK_LEN = 128
 
@@ -180,7 +181,7 @@
     )
     coeff_term = (coeff_local + coeff_carry) * norm_scale
     skip_term = skip_local * norm_scale
-    proj_sum, coeff_sum, skip_sum = lax.psum((proj_term, coeff_term, skip_term), ("tm", "dp"))
+    proj_sum, coeff_sum, skip_sum = psum(psum((proj_term, coeff_term, skip_term), "dp"), "tm")
     return (mixed[None], input_grad, proj_sum, coeff_sum, skip_sum)
 
 

time: 777 us -> 869 us (1.12)
  waiting for transfers between devices: 102 us -> 200 us
    psum x1 -> x2, waiting for transfers between devices: 61.4 us -> 178 us  [the longest x1 155 us: shards(): psum(psum((proj_term, coeff_term, skip_term), 'dp'), 'tm')]
    reduce_scatter x1, waiting for transfers between devices: 40.3 us -> 20.7 us  [shards(): lax.psum_scatter(partial_in[None], 'tensor', scatter_dimension=2, tiled=T...]
    psum x1 -> x2, blocking collectives: 29.1 us -> 23.8 us  [the longest x1 20.3 us: shards(): psum(psum((proj_term, coeff_term, skip_term), 'dp'), 'tm')]
  transfers between devices with their start and end apart: 3 -> 4, of which waited for: 2 -> 3; matrix products, arithmetic and copies ran while one was open for 2% -> 2% of each run, Pallas kernels for 0% -> 0%
where the time goes in v1:
time: 869 us; the launch traced here: 859 us
  matrix products  288 us (33%)
  waiting for transfers between devices  200 us (23%)
  other arithmetic  131 us (15%)
  blocking collectives  118 us (14%)
  local copies, waits for them, and re-layouts  103 us (12%)
  between operations  15.1 us (2%)
    psum x1, waiting for transfers between devices, shards(): psum(psum((proj_term, coeff_term, skip_term), 'dp'), 'tm')  155 us
    dot_general x18, matrix products, block_step(): jnp.einsum('mhts,shd->mhtd', kern_re * same_clip, block_in, precision=lar...  108 us
    dot_general x18, matrix products, block_step(): jnp.einsum('mhts,shd->mhtd', kern_im * same_clip, block_in, precision=lar...  102 us
    all_gather x7, blocking collectives, carried_in(): pieces = jax.tree.map(lambda part: lax.all_gather(part, axis), value)  94.2 us
    mul x6, other arithmetic, shards(): kern_im = damping * jnp.sin(angles[:, :, None, None] * lag_steps)  60.5 us
    reduce_sum x6, other arithmetic, block_step(): block_re[..., None] * state_im[:, :, None, :]  36.6 us
    dynamic_slice x36, local copies, waits for them, and re-layouts, intra(): lax.scan(jax.checkpoint(block_step), (initial, initial), (blocks_in, seg_...  30.8 us
    dot_general x6, matrix products, block_step(): jnp.einsum('ywo,ywlo->lwo', coefficient_imaginary, aggregate_imaginary, p...  27 us
  transfers between devices with their start and end apart: 4, of which 3 were waited for; matrix products, arithmetic and copies ran while one was open for 2% of the time, Pallas kernels for 0%

profile of v1, /device:TPU:0, one launch (start us, length us, event | category | flops | bytes accessed | tf_op | source)
XLA Modules:
  0.0 858.9 jit_solution(495196602819910565)
XLA Ops:
  13.1 14.9 %all-gather = f32[32,4,1]{2,0,1:T(8,128)S(1)} all-gather(f32[8,4,1]{2,0,1:T(8,128)S(1)} %get-tuple-element.1670), channel_id=2, replica_groups=mesh['group'=2,'tm'=4,'tensor'=2,'dp'=2] {'tm'}, dimensions={0}, use_global_device_ids=true | all-gather | bytes 640 | tf_op jit(solution)/shard_map/all_gather | solution.py:13
  28.2 13.3 %all-gather.1 = f32[32,4,1]{2,0,1:T(8,128)S(1)} all-gather(f32[8,4,1]{2,0,1:T(8,128)S(1)} %get-tuple-element.1669), channel_id=3, replica_groups=mesh['group'=2,'tm'=4,'tensor'=2,'dp'=2] {'tm'}, dimensions={0}, use_global_device_ids=true | all-gather | bytes 640 | tf_op jit(solution)/shard_map/all_gather | solution.py:13
  41.7 13.2 %all-gather.6 = f32[32,4,1]{2,0,1:T(8,128)S(1)} all-gather(f32[8,4,1]{2,0,1:T(8,128)S(1)} %neg.55), channel_id=8, replica_groups=mesh['group'=2,'tm'=4,'tensor'=2,'dp'=2] {'tm'}, dimensions={0}, use_global_device_ids=true | all-gather | bytes 640 | tf_op jit(solution)/shard_map/all_gather | solution.py:13
  79.2 146.0 %while.82 = (s32[]{:T(128)}, f32[8,4,128]{2,0,1:T(8,128)S(1)}, f32[8,4,128]{2,0,1:T(8,128)S(1)}, f32[6,128,4,128]{3,1,0,2:T(8,128)}, f32[6,8,4,128]{3,1,2,0:T(8,...) while((s32[]{:T(128)}, f32[8,4,128]{2,0,1:T(8,128)S(1)}, ...), condition=%wide.region_4.5_spmd.clone.clone, body=%wide.region_3.4_spmd.clone.clone.sunk | while | flops 1623294208 | bytes 7542485 | solution.py:125
  82.3 10.2 %multiply_reduce_fusion.11 = (f32[4,128,128]{1,2,0:T(8,128)S(1)}, f32[8,4,128,128]{3,2,0,1:T(8,128)S(1)}) fusion(f32[4,128,8]{1,2,0:T(8,128)S(1)} %copy.360, f32[8,4,128]{2,0,1:T(8,128)S(1)} %get-tuple-element.2160, f32[8,4,128]{2,0,1:T(8,128)S(1)} %bitcast.427, f32[8,4,128]{2,0,1:T(8,128)S(1)} %get-tuple-element.2161, ...), kind=kOutput, calls=%fused_computation.88.clone.1 | convolution fusion | flops 811532288 | bytes 2851584 | tf_op jit(solution)/shard_map/jvp()/while/body/eval_jaxpr/mhts,shd->mhtd/dot_general | solution.py:98
  92.5 10.3 %multiply_reduce_fusion.10 = (f32[4,128,128]{1,2,0:T(8,128)S(1)}, f32[8,4,128,128]{3,2,0,1:T(8,128)S(1)}) fusion(f32[4,128,8]{1,2,0:T(8,128)S(1)} %copy.359, f32[8,4,128]{2,0,1:T(8,128)S(1)} %get-tuple-element.2161, f32[8,4,128]{2,0,1:T(8,128)S(1)} %bitcast.428, f32[8,4,128]{2,0,1:T(8,128)S(1)} %get-tuple-element.2160, ...), kind=kOutput, calls=%fused_computation.89.clone.1 | convolution fusion | flops 811532288 | bytes 2851584 | tf_op jit(solution)/shard_map/jvp()/while/body/eval_jaxpr/mhts,shd->mhtd/dot_general | solution.py:95
  106.6 10.2 %multiply_reduce_fusion.11 = (f32[4,128,128]{1,2,0:T(8,128)S(1)}, f32[8,4,128,128]{3,2,0,1:T(8,128)S(1)}) fusion(f32[4,128,8]{1,2,0:T(8,128)S(1)} %copy.360, f32[8,4,128]{2,0,1:T(8,128)S(1)} %get-tuple-element.2160, f32[8,4,128]{2,0,1:T(8,128)S(1)} %bitcast.427, f32[8,4,128]{2,0,1:T(8,128)S(1)} %get-tuple-element.2161, ...), kind=kOutput, calls=%fused_computation.88.clone.1 | convolution fusion | flops 811532288 | bytes 2851584 | tf_op jit(solution)/shard_map/jvp()/while/body/eval_jaxpr/mhts,shd->mhtd/dot_general | solution.py:98
  116.8 10.3 %multiply_reduce_fusion.10 = (f32[4,128,128]{1,2,0:T(8,128)S(1)}, f32[8,4,128,128]{3,2,0,1:T(8,128)S(1)}) fusion(f32[4,128,8]{1,2,0:T(8,128)S(1)} %copy.359, f32[8,4,128]{2,0,1:T(8,128)S(1)} %get-tuple-element.2161, f32[8,4,128]{2,0,1:T(8,128)S(1)} %bitcast.428, f32[8,4,128]{2,0,1:T(8,128)S(1)} %get-tuple-element.2160, ...), kind=kOutput, calls=%fused_computation.89.clone.1 | convolution fusion | flops 811532288 | bytes 2851584 | tf_op jit(solution)/shard_map/jvp()/while/body/eval_jaxpr/mhts,shd->mhtd/dot_general | solution.py:95
  130.8 10.2 %multiply_reduce_fusion.11 = (f32[4,128,128]{1,2,0:T(8,128)S(1)}, f32[8,4,128,128]{3,2,0,1:T(8,128)S(1)}) fusion(f32[4,128,8]{1,2,0:T(8,128)S(1)} %copy.360, f32[8,4,128]{2,0,1:T(8,128)S(1)} %get-tuple-element.2160, f32[8,4,128]{2,0,1:T(8,128)S(1)} %bitcast.427, f32[8,4,128]{2,0,1:T(8,128)S(1)} %get-tuple-element.2161, ...), kind=kOutput, calls=%fused_computation.88.clone.1 | convolution fusion | flops 811532288 | bytes 2851584 | tf_op jit(solution)/shard_map/jvp()/while/body/eval_jaxpr/mhts,shd->mhtd/dot_general | solution.py:98
  141.0 10.3 %multiply_reduce_fusion.10 = (f32[4,128,128]{1,2,0:T(8,128)S(1)}, f32[8,4,128,128]{3,2,0,1:T(8,128)S(1)}) fusion(f32[4,128,8]{1,2,0:T(8,128)S(1)} %copy.359, f32[8,4,128]{2,0,1:T(8,128)S(1)} %get-tuple-element.2161, f32[8,4,128]{2,0,1:T(8,128)S(1)} %bitcast.428, f32[8,4,128]{2,0,1:T(8,128)S(1)} %get-tuple-element.2160, ...), kind=kOutput, calls=%fused_computation.89.clone.1 | convolution fusion | flops 811532288 | bytes 2851584 | tf_op jit(solution)/shard_map/jvp()/while/body/eval_jaxpr/mhts,shd->mhtd/dot_general | solution.py:95
  155.0 10.2 %multiply_reduce_fusion.11 = (f32[4,128,128]{1,2,0:T(8,128)S(1)}, f32[8,4,128,128]{3,2,0,1:T(8,128)S(1)}) fusion(f32[4,128,8]{1,2,0:T(8,128)S(1)} %copy.360, f32[8,4,128]{2,0,1:T(8,128)S(1)} %get-tuple-element.2160, f32[8,4,128]{2,0,1:T(8,128)S(1)} %bitcast.427, f32[8,4,128]{2,0,1:T(8,128)S(1)} %get-tuple-element.2161, ...), kind=kOutput, calls=%fused_computation.88.clone.1 | convolution fusion | flops 811532288 | bytes 2851584 | tf_op jit(solution)/shard_map/jvp()/while/body/eval_jaxpr/mhts,shd->mhtd/dot_general | solution.py:98
  165.2 10.3 %multiply_reduce_fusion.10 = (f32[4,128,128]{1,2,0:T(8,128)S(1)}, f32[8,4,128,128]{3,2,0,1:T(8,128)S(1)}) fusion(f32[4,128,8]{1,2,0:T(8,128)S(1)} %copy.359, f32[8,4,128]{2,0,1:T(8,128)S(1)} %get-tuple-element.2161, f32[8,4,128]{2,0,1:T(8,128)S(1)} %bitcast.428, f32[8,4,128]{2,0,1:T(8,128)S(1)} %get-tuple-element.2160, ...), kind=kOutput, calls=%fused_computation.89.clone.1 | convolution fusion | flops 811532288 | bytes 2851584 | tf_op jit(solution)/shard_map/jvp()/while/body/eval_jaxpr/mhts,shd->mhtd/dot_general | solution.py:95
  179.2 10.2 %multiply_reduce_fusion.11 = (f32[4,128,128]{1,2,0:T(8,128)S(1)}, f32[8,4,128,128]{3,2,0,1:T(8,128)S(1)}) fusion(f32[4,128,8]{1,2,0:T(8,128)S(1)} %copy.360, f32[8,4,128]{2,0,1:T(8,128)S(1)} %get-tuple-element.2160, f32[8,4,128]{2,0,1:T(8,128)S(1)} %bitcast.427, f32[8,4,128]{2,0,1:T(8,128)S(1)} %get-tuple-element.2161, ...), kind=kOutput, calls=%fused_computation.88.clone.1 | convolution fusion | flops 811532288 | bytes 2851584 | tf_op jit(solution)/shard_map/jvp()/while/body/eval_jaxpr/mhts,shd->mhtd/dot_general | solution.py:98
  189.4 10.3 %multiply_reduce_fusion.10 = (f32[4,128,128]{1,2,0:T(8,128)S(1)}, f32[8,4,128,128]{3,2,0,1:T(8,128)S(1)}) fusion(f32[4,128,8]{1,2,0:T(8,128)S(1)} %copy.359, f32[8,4,128]{2,0,1:T(8,128)S(1)} %get-tuple-element.2161, f32[8,4,128]{2,0,1:T(8,128)S(1)} %bitcast.428, f32[8,4,128]{2,0,1:T(8,128)S(1)} %get-tuple-element.2160, ...), kind=kOutput, calls=%fused_computation.89.clone.1 | convolution fusion | flops 811532288 | bytes 2851584 | tf_op jit(solution)/shard_map/jvp()/while/body/eval_jaxpr/mhts,shd->mhtd/dot_general | solution.py:95
  203.5 10.2 %multiply_reduce_fusion.11 = (f32[4,128,128]{1,2,0:T(8,128)S(1)}, f32[8,4,128,128]{3,2,0,1:T(8,128)S(1)}) fusion(f32[4,128,8]{1,2,0:T(8,128)S(1)} %copy.360, f32[8,4,128]{2,0,1:T(8,128)S(1)} %get-tuple-element.2160, f32[8,4,128]{2,0,1:T(8,128)S(1)} %bitcast.427, f32[8,4,128]{2,0,1:T(8,128)S(1)} %get-tuple-element.2161, ...), kind=kOutput, calls=%fused_computation.88.clone.1 | convolution fusion | flops 811532288 | bytes 2851584 | tf_op jit(solution)/shard_map/jvp()/while/body/eval_jaxpr/mhts,shd->mhtd/dot_general | solution.py:98
  213.7 10.3 %multiply_reduce_fusion.10 = (f32[4,128,128]{1,2,0:T(8,128)S(1)}, f32[8,4,128,128]{3,2,0,1:T(8,128)S(1)}) fusion(f32[4,128,8]{1,2,0:T(8,128)S(1)} %copy.359, f32[8,4,128]{2,0,1:T(8,128)S(1)} %get-tuple-element.2161, f32[8,4,128]{2,0,1:T(8,128)S(1)} %bitcast.428, f32[8,4,128]{2,0,1:T(8,128)S(1)} %get-tuple-element.2160, ...), kind=kOutput, calls=%fused_computation.89.clone.1 | convolution fusion | flops 811532288 | bytes 2851584 | tf_op jit(solution)/shard_map/jvp()/while/body/eval_jaxpr/mhts,shd->mhtd/dot_general | solution.py:95
  228.2 13.2 %all-gather.2 = f32[32,4,128]{2,0,1:T(8,128)S(1)} all-gather(f32[8,4,128]{2,0,1:T(8,128)S(1)} %get-tuple-element.821), channel_id=4, replica_groups=mesh['group'=2,'tm'=4,'tensor'=2,'dp'=2] {'tm'}, dimensions={0}, use_global_device_ids=true | all-gather | bytes 81920 | tf_op jit(solution)/shard_map/all_gather | solution.py:13
  241.4 13.2 %all-gather.3 = f32[32,4,128]{2,0,1:T(8,128)S(1)} all-gather(f32[8,4,128]{2,0,1:T(8,128)S(1)} %get-tuple-element.822), channel_id=5, replica_groups=mesh['group'=2,'tm'=4,'tensor'=2,'dp'=2] {'tm'}, dimensions={0}, use_global_device_ids=true | all-gather | bytes 81920 | tf_op jit(solution)/shard_map/all_gather | solution.py:13
  261.2 13.2 %all-gather.4 = f32[32,4,128]{2,0,1:T(8,128)S(1)} all-gather(f32[8,4,128]{2,0,1:T(8,128)S(1)} %get-tuple-element.1702), channel_id=6, replica_groups=mesh['group'=2,'tm'=4,'tensor'=2,'dp'=2] {'tm'}, dimensions={0}, use_global_device_ids=true | all-gather | bytes 81920 | tf_op jit(solution)/shard_map/all_gather | solution.py:13
  274.5 13.2 %all-gather.5 = f32[32,4,128]{2,0,1:T(8,128)S(1)} all-gather(f32[8,4,128]{2,0,1:T(8,128)S(1)} %get-tuple-element.1666), channel_id=7, replica_groups=mesh['group'=2,'tm'=4,'tensor'=2,'dp'=2] {'tm'}, dimensions={0}, use_global_device_ids=true | all-gather | bytes 81920 | tf_op jit(solution)/shard_map/all_gather | solution.py:13
  290.9 312.5 %while.83 = (s32[]{:T(128)}, f32[4,128]{1,0:T(4,128)S(1)}, f32[8,4,128]{2,1,0:T(4,128)}, f32[8,4,128]{2,1,0:T(4,128)}, f32[8,4,128]{2,0,1:T(8,128)}, /*index=5*/...) while((s32[]{:T(128)}, f32[4,128]{1,0:T(4,128)S(1)}, ...), condition=%wide.region_15.16_spmd.clone.clone.clone, body=%wide.region_9.15_spmd.clone.clone.clone.sunk | while | flops 3254166272 | bytes 45512152 | solution.py:125
  291.1 10.1 %fusion.192 = (f32[8,4,128,128]{3,2,0,1:T(8,128)}, f32[8,4,128,128]{3,2,0,1:T(8,128)}) fusion(f32[8,4]{0,1:T(4,128)S(1)} %get-tuple-element.2328, f32[128,128]{1,0:T(8,128)} %get-tuple-element.2327, f32[8,4]{0,1:T(4,128)S(1)} %get-tuple-element.2325, pred[128,128]{1,0:T(8,128)(4,1)S(1)} %get-tuple-element.2326), kind=kLoop, calls=%fused_computation.23.clone.1 | loop fusion | flops 2621440 | bytes 4276480 | tf_op jit(solution)/shard_map/mul | solution.py:58
  307.6 4.1 bitcast_add_fusion.17
  311.8 4.5 fusion.194
  316.4 4.2 bitcast_add_fusion.18
  320.6 4.5 fusion.195
  329.4 6.1 multiply_reduce_fusion.12
  343.2 10.1 %fusion.192 = (f32[8,4,128,128]{3,2,0,1:T(8,128)}, f32[8,4,128,128]{3,2,0,1:T(8,128)}) fusion(f32[8,4]{0,1:T(4,128)S(1)} %get-tuple-element.2328, f32[128,128]{1,0:T(8,128)} %get-tuple-element.2327, f32[8,4]{0,1:T(4,128)S(1)} %get-tuple-element.2325, pred[128,128]{1,0:T(8,128)(4,1)S(1)} %get-tuple-element.2326), kind=kLoop, calls=%fused_computation.23.clone.1 | loop fusion | flops 2621440 | bytes 4276480 | tf_op jit(solution)/shard_map/mul | solution.py:58
  359.7 4.1 bitcast_add_fusion.17
  363.8 4.5 fusion.194
  368.4 4.2 bitcast_add_fusion.18
  372.6 4.5 fusion.195
  381.4 6.1 multiply_reduce_fusion.12
  395.2 10.1 %fusion.192 = (f32[8,4,128,128]{3,2,0,1:T(8,128)}, f32[8,4,128,128]{3,2,0,1:T(8,128)}) fusion(f32[8,4]{0,1:T(4,128)S(1)} %get-tuple-element.2328, f32[128,128]{1,0:T(8,128)} %get-tuple-element.2327, f32[8,4]{0,1:T(4,128)S(1)} %get-tuple-element.2325, pred[128,128]{1,0:T(8,128)(4,1)S(1)} %get-tuple-element.2326), kind=kLoop, calls=%fused_computation.23.clone.1 | loop fusion | flops 2621440 | bytes 4276480 | tf_op jit(solution)/shard_map/mul | solution.py:58
  411.7 4.1 bitcast_add_fusion.17
  415.8 4.5 fusion.194
  420.4 4.2 bitcast_add_fusion.18
  424.7 4.5 fusion.195
  433.4 6.1 multiply_reduce_fusion.12
  447.2 10.1 %fusion.192 = (f32[8,4,128,128]{3,2,0,1:T(8,128)}, f32[8,4,128,128]{3,2,0,1:T(8,128)}) fusion(f32[8,4]{0,1:T(4,128)S(1)} %get-tuple-element.2328, f32[128,128]{1,0:T(8,128)} %get-tuple-element.2327, f32[8,4]{0,1:T(4,128)S(1)} %get-tuple-element.2325, pred[128,128]{1,0:T(8,128)(4,1)S(1)} %get-tuple-element.2326), kind=kLoop, calls=%fused_computation.23.clone.1 | loop fusion | flops 2621440 | bytes 4276480 | tf_op jit(solution)/shard_map/mul | solution.py:58
  463.7 4.1 bitcast_add_fusion.17
  467.8 4.5 fusion.194
  472.4 4.2 bitcast_add_fusion.18
  476.7 4.5 fusion.195
  485.4 6.1 multiply_reduce_fusion.12
  499.3 10.1 %fusion.192 = (f32[8,4,128,128]{3,2,0,1:T(8,128)}, f32[8,4,128,128]{3,2,0,1:T(8,128)}) fusion(f32[8,4]{0,1:T(4,128)S(1)} %get-tuple-element.2328, f32[128,128]{1,0:T(8,128)} %get-tuple-element.2327, f32[8,4]{0,1:T(4,128)S(1)} %get-tuple-element.2325, pred[128,128]{1,0:T(8,128)(4,1)S(1)} %get-tuple-element.2326), kind=kLoop, calls=%fused_computation.23.clone.1 | loop fusion | flops 2621440 | bytes 4276480 | tf_op jit(solution)/shard_map/mul | solution.py:58
  515.7 4.1 bitcast_add_fusion.17
  519.9 4.5 fusion.194
  524.5 4.2 bitcast_add_fusion.18
  528.7 4.5 fusion.195
  537.5 6.1 multiply_reduce_fusion.12
  551.3 10.1 %fusion.192 = (f32[8,4,128,128]{3,2,0,1:T(8,128)}, f32[8,4,128,128]{3,2,0,1:T(8,128)}) fusion(f32[8,4]{0,1:T(4,128)S(1)} %get-tuple-element.2328, f32[128,128]{1,0:T(8,128)} %get-tuple-element.2327, f32[8,4]{0,1:T(4,128)S(1)} %get-tuple-element.2325, pred[128,128]{1,0:T(8,128)(4,1)S(1)} %get-tuple-element.2326), kind=kLoop, calls=%fused_computation.23.clone.1 | loop fusion | flops 2621440 | bytes 4276480 | tf_op jit(solution)/shard_map/mul | solution.py:58
  567.8 4.1 bitcast_add_fusion.17
  571.9 4.5 fusion.194
  576.5 4.2 bitcast_add_fusion.18
  580.8 4.5 fusion.195
  589.5 6.1 multiply_reduce_fusion.12
  607.5 5.7 multiply_bitcast_fusion
  614.3 4.7 convolution_bitcast_fusion
  619.1 23.6 %all-reduce.11.cloned.1.call-done = f32[2,1024,512]{1,2,0:T(8,128)} async-done(((f32[2,1024,512]{1,2,0:T(8,128)}), f32[2,1024,512]{1,2,0:T(8,128)}) %all-reduce.11.cloned.1.call-update) | async-done | bytes 4194320 | tf_op jit(solution)/shard_map/psum | solution.py:184
  648.5 20.3 %all-reduce.6 = (f32[2,8,512]{2,1,0:T(8,128)}, f32[512]{0:T(512)}) all-reduce(f32[2,8,512]{2,1,0:T(8,128)S(1)} %get-tuple-element.1662, f32[512]{0:T(512)S(1)} %get-tuple-element.1663), channel_id=1, replica_groups=mesh['group'=2,'tm'=4,'tensor'=2,'dp'=2] {'tm'}, use_global_device_ids=true, to_apply=%region_20.21 | all-reduce | flops 8704 | bytes 69632 | tf_op jit(solution)/shard_map/psum | solution.py:184
  668.8 20.7 %reduce-scatter.2.cloned.1.call-done = f32[1,768,512]{2,1,0:T(8,128)} async-done(((f32[1,768,1024]{2,1,0:T(8,128)}), f32[1,768,512]{2,1,0:T(8,128)}) %reduce-scatter.2.cloned.1.call-update) | async-done | bytes 1572880 | tf_op jit(solution)/shard_map/reduce_scatter | solution.py:174
  691.9 154.8 %all-reduce.13.cloned.1.call-done = f32[2,1024,512]{1,2,0:T(8,128)} async-done(((f32[2,1024,512]{1,2,0:T(8,128)}), f32[2,1024,512]{1,2,0:T(8,128)}) %all-reduce.13.cloned.1.call-update) | async-done | bytes 4194320 | tf_op jit(solution)/shard_map/psum | solution.py:184
  846.8 5.4 copy.231
  (651 shorter events, 188.6 us)
Async XLA Ops:
  7.2 48.9 %copy-start = (bf16[2,1024,512]{2,1,0:T(8,128)(2,1)S(1)}, bf16[2,1024,512]{2,1,0:T(8,128)(2,1)}, u32[]{:S(2)}) copy-start(bf16[2,1024,512]{2,1,0:T(8,128)(2,1)} %param.17) | copy-start | bytes 6291460
  7.2 48.9 %all-gather.9.cloned.1.call-start = ((), (), s32[]{:S(2)}) async-start(), calls=%async_computation.1 | async-start | bytes 2359296 | tf_op jit(solution)/shard_map/all_gather | solution.py:46
  7.9 634.7 %all-reduce.11.cloned.1.call-start = ((), (), s32[]{:S(2)}) async-start(), calls=%async_computation.3 | async-start | bytes 8388608 | tf_op jit(solution)/shard_map/psum | solution.py:184
  11.8 248.7 %copy-start.38 = (f32[8,4]{0,1:T(4,128)}, f32[8,4]{0,1:T(4,128)S(1)}, u32[]{:S(2)}) copy-start(f32[8,4]{0,1:T(4,128)S(1)} %get-tuple-element.1707) | copy-start | bytes 388
  260.5 30.4 %copy-start.31 = (f32[4,128]{1,0:T(4,128)S(1)}, f32[4,128]{1,0:T(4,128)}, u32[]{:S(2)}) copy-start(f32[4,128]{1,0:T(4,128)} %custom-call.4) | copy-start | bytes 6148
  291.1 10.1 %copy-start.11 = (pred[128,128]{1,0:T(8,128)(4,1)}, pred[128,128]{1,0:T(8,128)(4,1)S(1)}, u32[]{:S(2)}) copy-start(pred[128,128]{1,0:T(8,128)(4,1)S(1)} %get-tuple-element.2326) | copy-start | bytes 49156 | tf_op jit(solution)/shard_map/transpose(jvp())/while
  291.1 10.1 %copy-start.21 = (f32[8,4]{0,1:T(4,128)}, f32[8,4]{0,1:T(4,128)S(1)}, u32[]{:S(2)}) copy-start(f32[8,4]{0,1:T(4,128)S(1)} %get-tuple-element.2325) | copy-start | bytes 388 | tf_op jit(solution)/shard_map/transpose(jvp())/while
  291.1 10.1 %copy-start.24 = (f32[8,4]{0,1:T(4,128)}, f32[8,4]{0,1:T(4,128)S(1)}, u32[]{:S(2)}) copy-start(f32[8,4]{0,1:T(4,128)S(1)} %get-tuple-element.2328) | copy-start | bytes 388 | tf_op jit(solution)/shard_map/transpose(jvp())/while
  291.1 10.1 %copy-start.27 = (f32[4,128]{1,0:T(4,128)}, f32[4,128]{1,0:T(4,128)S(1)}, u32[]{:S(2)}) copy-start(f32[4,128]{1,0:T(4,128)S(1)} %get-tuple-element.2139) | copy-start | bytes 6148 | tf_op jit(solution)/shard_map/transpose(jvp())/while
  291.1 12.7 %copy-start.40 = (s32[6,128]{1,0:T(8,128)}, s32[6,128]{1,0:T(8,128)S(1)}, u32[]{:S(2)}) copy-start(s32[6,128]{1,0:T(8,128)S(1)} %get-tuple-element.2317) | copy-start | bytes 9220 | tf_op jit(solution)/shard_map/transpose(jvp())/while
  291.1 12.7 %copy-start.45 = (s32[6]{0:T(128)}, s32[6]{0:T(128)S(1)}, u32[]{:S(2)}) copy-start(s32[6]{0:T(128)S(1)} %get-tuple-element.2318) | copy-start | bytes 76 | tf_op jit(solution)/shard_map/transpose(jvp())/while
  329.3 7.3 copy-start.1
  329.3 7.3 copy-start.2
  329.3 7.3 copy-start.28
  343.1 10.1 %copy-start.11 = (pred[128,128]{1,0:T(8,128)(4,1)}, pred[128,128]{1,0:T(8,128)(4,1)S(1)}, u32[]{:S(2)}) copy-start(pred[128,128]{1,0:T(8,128)(4,1)S(1)} %get-tuple-element.2326) | copy-start | bytes 49156 | tf_op jit(solution)/shard_map/transpose(jvp())/while
  343.1 10.1 %copy-start.21 = (f32[8,4]{0,1:T(4,128)}, f32[8,4]{0,1:T(4,128)S(1)}, u32[]{:S(2)}) copy-start(f32[8,4]{0,1:T(4,128)S(1)} %get-tuple-element.2325) | copy-start | bytes 388 | tf_op jit(solution)/shard_map/transpose(jvp())/while
  343.1 10.1 %copy-start.24 = (f32[8,4]{0,1:T(4,128)}, f32[8,4]{0,1:T(4,128)S(1)}, u32[]{:S(2)}) copy-start(f32[8,4]{0,1:T(4,128)S(1)} %get-tuple-element.2328) | copy-start | bytes 388 | tf_op jit(solution)/shard_map/transpose(jvp())/while
  343.1 10.1 %copy-start.27 = (f32[4,128]{1,0:T(4,128)}, f32[4,128]{1,0:T(4,128)S(1)}, u32[]{:S(2)}) copy-start(f32[4,128]{1,0:T(4,128)S(1)} %get-tuple-element.2139) | copy-start | bytes 6148 | tf_op jit(solution)/shard_map/transpose(jvp())/while
  343.1 12.7 %copy-start.40 = (s32[6,128]{1,0:T(8,128)}, s32[6,128]{1,0:T(8,128)S(1)}, u32[]{:S(2)}) copy-start(s32[6,128]{1,0:T(8,128)S(1)} %get-tuple-element.2317) | copy-start | bytes 9220 | tf_op jit(solution)/shard_map/transpose(jvp())/while
  343.2 12.7 %copy-start.45 = (s32[6]{0:T(128)}, s32[6]{0:T(128)S(1)}, u32[]{:S(2)}) copy-start(s32[6]{0:T(128)S(1)} %get-tuple-element.2318) | copy-start | bytes 76 | tf_op jit(solution)/shard_map/transpose(jvp())/while
  381.4 7.3 copy-start.1
  381.4 7.3 copy-start.2
  381.4 7.3 copy-start.28
  395.1 10.1 %copy-start.11 = (pred[128,128]{1,0:T(8,128)(4,1)}, pred[128,128]{1,0:T(8,128)(4,1)S(1)}, u32[]{:S(2)}) copy-start(pred[128,128]{1,0:T(8,128)(4,1)S(1)} %get-tuple-element.2326) | copy-start | bytes 49156 | tf_op jit(solution)/shard_map/transpose(jvp())/while
  395.2 10.1 %copy-start.21 = (f32[8,4]{0,1:T(4,128)}, f32[8,4]{0,1:T(4,128)S(1)}, u32[]{:S(2)}) copy-start(f32[8,4]{0,1:T(4,128)S(1)} %get-tuple-element.2325) | copy-start | bytes 388 | tf_op jit(solution)/shard_map/transpose(jvp())/while
  395.2 10.1 %copy-start.24 = (f32[8,4]{0,1:T(4,128)}, f32[8,4]{0,1:T(4,128)S(1)}, u32[]{:S(2)}) copy-start(f32[8,4]{0,1:T(4,128)S(1)} %get-tuple-element.2328) | copy-start | bytes 388 | tf_op jit(solution)/shard_map/transpose(jvp())/while
  395.2 10.1 %copy-start.27 = (f32[4,128]{1,0:T(4,128)}, f32[4,128]{1,0:T(4,128)S(1)}, u32[]{:S(2)}) copy-start(f32[4,128]{1,0:T(4,128)S(1)} %get-tuple-element.2139) | copy-start | bytes 6148 | tf_op jit(solution)/shard_map/transpose(jvp())/while
  395.2 12.7 %copy-start.40 = (s32[6,128]{1,0:T(8,128)}, s32[6,128]{1,0:T(8,128)S(1)}, u32[]{:S(2)}) copy-start(s32[6,128]{1,0:T(8,128)S(1)} %get-tuple-element.2317) | copy-start | bytes 9220 | tf_op jit(solution)/shard_map/transpose(jvp())/while
  395.2 12.7 %copy-start.45 = (s32[6]{0:T(128)}, s32[6]{0:T(128)S(1)}, u32[]{:S(2)}) copy-start(s32[6]{0:T(128)S(1)} %get-tuple-element.2318) | copy-start | bytes 76 | tf_op jit(solution)/shard_map/transpose(jvp())/while
  424.7 6.7 copy-start.13
  433.4 7.3 copy-start.1
  433.4 7.3 copy-start.2
  433.4 7.3 copy-start.28
  447.2 10.1 %copy-start.11 = (pred[128,128]{1,0:T(8,128)(4,1)}, pred[128,128]{1,0:T(8,128)(4,1)S(1)}, u32[]{:S(2)}) copy-start(pred[128,128]{1,0:T(8,128)(4,1)S(1)} %get-tuple-element.2326) | copy-start | bytes 49156 | tf_op jit(solution)/shard_map/transpose(jvp())/while
  447.2 10.1 %copy-start.21 = (f32[8,4]{0,1:T(4,128)}, f32[8,4]{0,1:T(4,128)S(1)}, u32[]{:S(2)}) copy-start(f32[8,4]{0,1:T(4,128)S(1)} %get-tuple-element.2325) | copy-start | bytes 388 | tf_op jit(solution)/shard_map/transpose(jvp())/while
  447.2 10.1 %copy-start.24 = (f32[8,4]{0,1:T(4,128)}, f32[8,4]{0,1:T(4,128)S(1)}, u32[]{:S(2)}) copy-start(f32[8,4]{0,1:T(4,128)S(1)} %get-tuple-element.2328) | copy-start | bytes 388 | tf_op jit(solution)/shard_map/transpose(jvp())/while
  447.2 10.1 %copy-start.27 = (f32[4,128]{1,0:T(4,128)}, f32[4,128]{1,0:T(4,128)S(1)}, u32[]{:S(2)}) copy-start(f32[4,128]{1,0:T(4,128)S(1)} %get-tuple-element.2139) | copy-start | bytes 6148 | tf_op jit(solution)/shard_map/transpose(jvp())/while
  447.2 12.7 %copy-start.40 = (s32[6,128]{1,0:T(8,128)}, s32[6,128]{1,0:T(8,128)S(1)}, u32[]{:S(2)}) copy-start(s32[6,128]{1,0:T(8,128)S(1)} %get-tuple-element.2317) | copy-start | bytes 9220 | tf_op jit(solution)/shard_map/transpose(jvp())/while
  447.2 12.7 %copy-start.45 = (s32[6]{0:T(128)}, s32[6]{0:T(128)S(1)}, u32[]{:S(2)}) copy-start(s32[6]{0:T(128)S(1)} %get-tuple-element.2318) | copy-start | bytes 76 | tf_op jit(solution)/shard_map/transpose(jvp())/while
  476.7 6.7 copy-start.13
  485.4 7.3 copy-start.1
  485.4 7.3 copy-start.2
  485.4 7.3 copy-start.28
  499.2 10.1 %copy-start.11 = (pred[128,128]{1,0:T(8,128)(4,1)}, pred[128,128]{1,0:T(8,128)(4,1)S(1)}, u32[]{:S(2)}) copy-start(pred[128,128]{1,0:T(8,128)(4,1)S(1)} %get-tuple-element.2326) | copy-start | bytes 49156 | tf_op jit(solution)/shard_map/transpose(jvp())/while
  499.2 10.1 %copy-start.21 = (f32[8,4]{0,1:T(4,128)}, f32[8,4]{0,1:T(4,128)S(1)}, u32[]{:S(2)}) copy-start(f32[8,4]{0,1:T(4,128)S(1)} %get-tuple-element.2325) | copy-start | bytes 388 | tf_op jit(solution)/shard_map/transpose(jvp())/while
  499.2 10.1 %copy-start.24 = (f32[8,4]{0,1:T(4,128)}, f32[8,4]{0,1:T(4,128)S(1)}, u32[]{:S(2)}) copy-start(f32[8,4]{0,1:T(4,128)S(1)} %get-tuple-element.2328) | copy-start | bytes 388 | tf_op jit(solution)/shard_map/transpose(jvp())/while
  499.2 10.1 %copy-start.27 = (f32[4,128]{1,0:T(4,128)}, f32[4,128]{1,0:T(4,128)S(1)}, u32[]{:S(2)}) copy-start(f32[4,128]{1,0:T(4,128)S(1)} %get-tuple-element.2139) | copy-start | bytes 6148 | tf_op jit(solution)/shard_map/transpose(jvp())/while
  499.2 12.7 %copy-start.40 = (s32[6,128]{1,0:T(8,128)}, s32[6,128]{1,0:T(8,128)S(1)}, u32[]{:S(2)}) copy-start(s32[6,128]{1,0:T(8,128)S(1)} %get-tuple-element.2317) | copy-start | bytes 9220 | tf_op jit(solution)/shard_map/transpose(jvp())/while
  499.2 12.7 %copy-start.45 = (s32[6]{0:T(128)}, s32[6]{0:T(128)S(1)}, u32[]{:S(2)}) copy-start(s32[6]{0:T(128)S(1)} %get-tuple-element.2318) | copy-start | bytes 76 | tf_op jit(solution)/shard_map/transpose(jvp())/while
  537.4 7.3 copy-start.1
  537.5 7.3 copy-start.2
  537.5 7.3 copy-start.28
  551.2 10.1 %copy-start.11 = (pred[128,128]{1,0:T(8,128)(4,1)}, pred[128,128]{1,0:T(8,128)(4,1)S(1)}, u32[]{:S(2)}) copy-start(pred[128,128]{1,0:T(8,128)(4,1)S(1)} %get-tuple-element.2326) | copy-start | bytes 49156 | tf_op jit(solution)/shard_map/transpose(jvp())/while
  551.2 10.1 %copy-start.21 = (f32[8,4]{0,1:T(4,128)}, f32[8,4]{0,1:T(4,128)S(1)}, u32[]{:S(2)}) copy-start(f32[8,4]{0,1:T(4,128)S(1)} %get-tuple-element.2325) | copy-start | bytes 388 | tf_op jit(solution)/shard_map/transpose(jvp())/while
  551.2 10.1 %copy-start.24 = (f32[8,4]{0,1:T(4,128)}, f32[8,4]{0,1:T(4,128)S(1)}, u32[]{:S(2)}) copy-start(f32[8,4]{0,1:T(4,128)S(1)} %get-tuple-element.2328) | copy-start | bytes 388 | tf_op jit(solution)/shard_map/transpose(jvp())/while
  551.2 10.1 %copy-start.27 = (f32[4,128]{1,0:T(4,128)}, f32[4,128]{1,0:T(4,128)S(1)}, u32[]{:S(2)}) copy-start(f32[4,128]{1,0:T(4,128)S(1)} %get-tuple-element.2139) | copy-start | bytes 6148 | tf_op jit(solution)/shard_map/transpose(jvp())/while
  551.3 12.7 %copy-start.40 = (s32[6,128]{1,0:T(8,128)}, s32[6,128]{1,0:T(8,128)S(1)}, u32[]{:S(2)}) copy-start(s32[6,128]{1,0:T(8,128)S(1)} %get-tuple-element.2317) | copy-start | bytes 9220 | tf_op jit(solution)/shard_map/transpose(jvp())/while
  551.3 12.7 %copy-start.45 = (s32[6]{0:T(128)}, s32[6]{0:T(128)S(1)}, u32[]{:S(2)}) copy-start(s32[6]{0:T(128)S(1)} %get-tuple-element.2318) | copy-start | bytes 76 | tf_op jit(solution)/shard_map/transpose(jvp())/while
  580.8 6.7 copy-start.13
  589.5 7.3 copy-start.1
  589.5 7.3 copy-start.2
  589.5 7.3 copy-start.28
  613.2 76.3 %reduce-scatter.2.cloned.1.call-start = ((), (), s32[]{:S(2)}) async-start(), calls=%async_computation.2 | async-start | bytes 4718592 | tf_op jit(solution)/shard_map/reduce_scatter | solution.py:174
  619.0 227.7 %all-reduce.13.cloned.1.call-start = ((), (), s32[]{:S(2)}) async-start(), calls=%async_computation.4 | async-start | bytes 8388608 | tf_op jit(solution)/shard_map/psum | solution.py:184
  (122 other events, 420.4 us)
Sparse Core Ops, SparseCore 0:
  9.6 29.8 all-gather.8
  613.3 29.2 all-reduce.10
  645.0 44.5 reduce-scatter.1
  691.7 154.9 all-reduce.12
